TPU v7x, 512 devices: a whole 4x8x8 slice. The times are simulated.
512 devices in a mesh: ctx: 128 (over y, z, x_lo), tp: 4 (over x_hi, core).
Axes of the slice: x: 4 (x_hi: 2, x_lo: 2; x = x_hi * 2 + x_lo), y: 8, z: 8, core: 2. Of those that a mesh axis runs over, the one named last changes fastest.
Arguments:
- features: bfloat16 [3, 2048, 16384], P(None, 'tp', 'ctx'), may hold values from -6 to 6
- short_taps: float32 [3, 3, 2048], P(None, None, 'tp'), may hold values from -3 to 3
- filters: bfloat16 [128, 16384], P('tp'), may hold values from -2 to 2
- skip_gain: float32 [2048], P('tp'), may hold values from -4 to 4
- out_weight: bfloat16 [2048, 2048], P('tp'), may hold values from -0.125 to 0.125
Outputs:
- block_out: bfloat16 [2048, 16384], P('tp', 'ctx')
All inputs are finite; a program needn't handle non-finite values.
Results may differ from a plain program's by a relative error of at most 0.009.
Values may be sent and summed in bfloat16 or wider, within the bound.
No kernel may reach another device: no remote copies, remote signals or barrier semaphores. Data moves between devices by JAX's collectives and lax.ppermute only.
A program may use at most 64 MiB of HBM per device.

v0:
```python
import math
import jax
import jax.numpy as jnp
from jax import lax
from jax.sharding import PartitionSpec as P

GROUP = 16
highest = lax.Precision.HIGHEST


def from_behind(value, axis, steps):
    count = lax.axis_size(axis)
    initial, last = (max(0, -steps), min(count, count - steps))
    return lax.ppermute(value, axis, [(source, source + steps) for source in range(initial, last)])


def left_product(matrix, stacked):
    return jnp.einsum("kn,bns->bks", matrix, stacked, precision=highest)


def right_product(stacked, matrix):
    return jnp.einsum("bks,st->bkt", stacked, matrix, precision=highest)


def split_length(total_len):
    row_count = 2
    for candidate in range(2, math.isqrt(total_len) + 1, 2):
        if total_len % candidate == 0:
            row_count = candidate
    return (row_count, total_len // row_count)


def dft_tables(row_count, col_count):
    total_len = row_count * col_count
    row_index = jnp.arange(row_count, dtype=jnp.int32)
    col_index = jnp.arange(col_count, dtype=jnp.int32)
    row_angle = (row_index[:, None] * row_index[None, :] % row_count).astype(jnp.float32) * (
        2.0 * math.pi / row_count
    )
    col_angle = (col_index[:, None] * col_index[None, :] % col_count).astype(jnp.float32) * (
        2.0 * math.pi / col_count
    )
    twist_angle = (row_index[:, None] * col_index[None, :] % total_len).astype(jnp.float32) * (
        2.0 * math.pi / total_len
    )
    return (
        jnp.cos(row_angle),
        jnp.sin(row_angle),
        jnp.cos(col_angle),
        jnp.sin(col_angle),
        jnp.cos(twist_angle),
        jnp.sin(twist_angle),
    )


def forward_dft(signal, tables):
    cos_row, sin_row, cos_col, sin_col, cos_twist, sin_twist = tables
    half_rows = signal.shape[1]
    first_real = left_product(cos_row[:, :half_rows], signal)
    first_imag = -left_product(sin_row[:, :half_rows], signal)
    twist_real = first_real * cos_twist + first_imag * sin_twist
    twist_imag = first_imag * cos_twist - first_real * sin_twist
    spec_real = right_product(twist_real, cos_col) + right_product(twist_imag, sin_col)
    spec_imag = right_product(twist_imag, cos_col) - right_product(twist_real, sin_col)
    return (spec_real, spec_imag)


def inverse_dft(spec_real, spec_imag, tables, half_rows):
    cos_row, sin_row, cos_col, sin_col, cos_twist, sin_twist = tables
    total_len = cos_row.shape[0] * cos_col.shape[0]
    middle_real = right_product(spec_real, cos_col) - right_product(spec_imag, sin_col)
    middle_imag = right_product(spec_imag, cos_col) + right_product(spec_real, sin_col)
    turned_real = middle_real * cos_twist - middle_imag * sin_twist
    turned_imag = middle_imag * cos_twist + middle_real * sin_twist
    signal = left_product(cos_row[:half_rows, :], turned_real) - left_product(
        sin_row[:half_rows, :], turned_imag
    )
    return signal / total_len


def local(features, short_taps, filters, skip_gain, out_weight):
    taps_count = short_taps.shape[0]
    chan_tp = features.shape[1]
    tok_local = features.shape[2]
    ctx_count = lax.axis_size("ctx")
    chan_dev = chan_tp // ctx_count
    group_dev = max(1, chan_dev // GROUP)
    per_group = chan_dev // group_dev
    seq_len = tok_local * ctx_count
    row_count, col_count = split_length(2 * seq_len)
    half_rows = row_count // 2
    tables = dft_tables(row_count, col_count)
    ctx_rank = lax.axis_index("ctx")
    kernel_rows = lax.dynamic_slice_in_dim(filters, ctx_rank * chan_dev // GROUP, group_dev, 0)
    kernel_real, kernel_imag = forward_dft(
        kernel_rows.astype(jnp.float32).reshape(group_dev, half_rows, col_count), tables
    )
    previous = from_behind(features[:, :, tok_local - (taps_count - 1) :], "ctx", 1)
    extended = jnp.concatenate([previous, features], axis=2).astype(jnp.float32)
    conv_all = jnp.zeros(features.shape, jnp.float32)
    for offset in range(taps_count):
        begin_at = taps_count - 1 - offset
        conv_all = (
            conv_all
            + short_taps[offset][:, :, None] * extended[:, :, begin_at : begin_at + tok_local]
        )
    query_conv = conv_all[0]
    product = (conv_all[1] * conv_all[2]).astype(jnp.bfloat16)
    gathered = lax.all_to_all(product, "ctx", split_axis=0, concat_axis=1, tiled=True)
    signal = gathered.astype(jnp.float32)
    sig_real, sig_imag = forward_dft(signal.reshape(chan_dev, half_rows, col_count), tables)
    four_shape = (group_dev, per_group, row_count, col_count)
    sig_real = sig_real.reshape(four_shape)
    sig_imag = sig_imag.reshape(four_shape)
    kernel_wide_real = kernel_real[:, None]
    kernel_wide_imag = kernel_imag[:, None]
    prod_real = (sig_real * kernel_wide_real - sig_imag * kernel_wide_imag).reshape(
        chan_dev, row_count, col_count
    )
    prod_imag = (sig_real * kernel_wide_imag + sig_imag * kernel_wide_real).reshape(
        chan_dev, row_count, col_count
    )
    longconv = inverse_dft(prod_real, prod_imag, tables, half_rows).reshape(chan_dev, seq_len)
    skip_local = lax.dynamic_slice_in_dim(skip_gain, ctx_rank * chan_dev, chan_dev, 0)
    long_mix = (longconv + skip_local[:, None] * signal).astype(jnp.bfloat16)
    restored = lax.all_to_all(long_mix, "ctx", split_axis=1, concat_axis=0, tiled=True)
    gated = (query_conv * restored.astype(jnp.float32)).astype(jnp.bfloat16)
    return lax.psum_scatter(
        lax.dot_general(
            out_weight, gated, (((0,), (0,)), ((), ())), preferred_element_type=jnp.float32
        ).astype(jnp.bfloat16),
        "tp",
        scatter_dimension=0,
        tiled=True,
    )


def solution(mesh):
    placed = (P(None, "tp", "ctx"), P(None, None, "tp"), P("tp", None), P("tp"), P("tp", None))
    return jax.shard_map(
        local, mesh=mesh, in_specs=placed, out_specs=P("tp", "ctx"), check_vma=False
    )
```

profile of v0, /device:TPU:1, one launch (start us, length us, event | category | flops | bytes accessed | tf_op | source)
XLA Modules:
  0.0 139.9 jit_solution(3832880754229626524)
XLA Ops:
  6.5 0.0 copy-start
  6.5 2.1 %slice.49 = bf16[3,512,2]{2,1,0:T(8,128)(2,1)} slice(bf16[3,512,128]{2,1,0:T(8,128)(2,1)} %param.5), slice={[0:3], [0:512], [126:128]} | slice | bytes 12288 | tf_op jit(solution)/shard_map/slice | solution.py:98
  8.6 3.9 %collective-permute-start = (bf16[3,512,2]{2,1,0:T(8,128)(2,1)}, bf16[3,512,2]{2,1,0:T(8,128)(2,1)S(1)}, u32[]{:S(2)}, u32[]{:S(2)}) collective-permute-start(bf16[3,512,2]{2,1,0:T(8,128)(2,1)} %slice.49), channel_id=1, source_target_pairs={{0,4},{4,8},{8,12},{12,16},{16,20},{20,24},{24,28},{28,32},{32,36}... | collective-permute-start | bytes 18440 | tf_op jit(solution)/shard_map/ppermute | solution.py:14
  12.6 0.3 fusion.85
  12.8 0.0 copy-start.2
  12.8 0.3 fusion.84
  13.1 1.2 dynamic-slice_reduce_fusion
  14.3 0.3 fusion.4
  14.6 0.3 convolution_bitcast_fusion.1
  14.9 1.8 %fusion.46 = f32[128,256]{1,0:T(8,128)S(1)} fusion(f32[1,128,256]{1,2,0:T(8,128)S(1)} %convolution_bitcast_fusion.1, f32[1,128,256]{1,2,0:T(8,128)S(1)} %fusion.4), kind=kOutput, calls=%fused_computation.77 | convolution fusion | flops 102137856 | bytes 393216 | tf_op jit(solution)/shard_map/bks,st->bkt/dot_general | solution.py:22
  16.7 0.0 copy-start.8
  16.7 0.0 copy-start.1
  16.7 2.5 %fusion.50 = f32[128,256]{1,0:T(8,128)} fusion(f32[1,128,256]{1,2,0:T(8,128)S(1)} %fusion.4, f32[1,128,256]{1,2,0:T(8,128)S(1)} %convolution_bitcast_fusion.1), kind=kOutput, calls=%fused_computation.81 | convolution fusion | flops 102137856 | bytes 393216 | tf_op jit(solution)/shard_map/bks,st->bkt/dot_general | solution.py:22
  19.2 0.0 copy-done.6
  19.2 1.8 %convolution_subtract_fusion.3 = f32[128,256]{1,0:T(8,128)S(1)} fusion(f32[128,256]{1,0:T(8,128)S(1)} %fusion.46, f32[1,128,256]{1,2,0:T(8,128)S(1)} %fusion.4, f32[1,128,256]{1,2,0:T(8,128)S(1)} %convolution_bitcast_fusion.1), kind=kOutput, calls=%fused_computation.12 | convolution fusion | flops 102170624 | bytes 524288 | tf_op jit(solution)/shard_map/bks,st->bkt/dot_general | solution.py:22
  21.0 0.0 collective-permute-done
  21.1 0.3 maximum_convert_fusion
  21.4 1.2 fusion.5
  22.6 0.7 fusion.17
  23.3 20.1 %all-to-all-start = ((bf16[128,4,128]{2,1,0:T(4,128)(2,1)}), bf16[128,4,128]{2,1,0:T(4,128)(2,1)S(1)}, u32[]{:S(2)}, u32[]{:S(2)}) async-start(bf16[128,4,128]{2,1,0:T(4,128)(2,1)} %bitcast.4), calls=%async_computation | async-start | bytes 262144 | tf_op jit(solution)/shard_map/all_to_all | solution.py:109
  43.3 0.2 reduce-scatter.2.cloned.1.call-start
  43.6 0.5 fusion.77
  44.1 0.8 dynamic_slice.7
  44.9 2.8 %convolution_add_fusion.2 = f32[128,256]{1,0:T(8,128)S(1)} fusion(f32[128,256]{1,0:T(8,128)} %fusion.50, f32[1,128,256]{1,2,0:T(8,128)} %copy-done.7, f32[1,128,256]{1,2,0:T(8,128)} %copy-done.6), kind=kOutput, calls=%fused_computation.13 | convolution fusion | flops 102170624 | bytes 524288 | tf_op jit(solution)/shard_map/bks,st->bkt/dot_general | solution.py:22
  47.7 6.8 %all-to-all-done = bf16[128,4,128]{2,1,0:T(4,128)(2,1)S(1)} async-done(((bf16[128,4,128]{2,1,0:T(4,128)(2,1)}), bf16[128,4,128]{2,1,0:T(4,128)(2,1)S(1)}, u32[]{:S(2)}, u32[]{:S(2)}) %all-to-all-start) | async-done | bytes 131104 | tf_op jit(solution)/shard_map/all_to_all | solution.py:109
  54.5 0.7 copy.68
  55.2 1.6 %reshape.145 = bf16[4,64,256]{2,1,0:T(8,128)(2,1)} reshape(bf16[4,128,128]{2,1,0:T(8,128)(2,1)} %bitcast.84) | data formatting | bytes 262144 | tf_op jit(solution)/shard_map/reshape | solution.py:111
  56.8 1.3 fusion.1
  58.2 1.3 convolution_bitcast_fusion
  59.5 1.9 %fusion.28 = f32[4,128,256]{2,1,0:T(8,128)S(1)} fusion(f32[4,128,256]{1,2,0:T(8,128)S(1)} %convolution_bitcast_fusion, f32[4,128,256]{1,2,0:T(8,128)S(1)} %fusion.1, f32[128,256]{0,1:T(8,128)S(1)} %get-tuple-element.8, f32[128,256]{0,1:T(8,128)S(1)} %get-tuple-element.9), kind=kOutput, calls=%fused_computation.53 | convolution fusion | flops 403963904 | bytes 1835008 | tf_op jit(solution)/shard_map/bks,st->bkt/dot_general | solution.py:22
  61.4 1.9 %fusion.30 = f32[4,128,256]{2,1,0:T(8,128)S(1)} fusion(f32[4,128,256]{1,2,0:T(8,128)S(1)} %fusion.1, f32[4,128,256]{1,2,0:T(8,128)S(1)} %convolution_bitcast_fusion, f32[128,256]{0,1:T(8,128)S(1)} %get-tuple-element.8, f32[128,256]{0,1:T(8,128)S(1)} %get-tuple-element.9), kind=kOutput, calls=%fused_computation.55 | convolution fusion | flops 403963904 | bytes 1835008 | tf_op jit(solution)/shard_map/bks,st->bkt/dot_general | solution.py:22
  63.3 1.9 %convolution_subtract_fusion.1 = f32[4,128,256]{2,1,0:T(8,128)S(1)} fusion(f32[4,128,256]{2,1,0:T(8,128)S(1)} %fusion.28, f32[4,128,256]{1,2,0:T(8,128)S(1)} %fusion.1, f32[4,128,256]{1,2,0:T(8,128)S(1)} %convolution_bitcast_fusion, f32[128,256]{0,1:T(8,128)S(1)} %get-tuple-element.8, f32[128,256]{0,1:T(8,128)S(1)} %get-tuple-element.9), kind=kOutput, calls=%fused_computation.7 | convolution fusion | flops 404094976 | bytes 2359296 | tf_op jit(solution)/shard_map/bks,st->bkt/dot_general | solution.py:22
  65.2 1.9 %convolution_add_fusion.1 = f32[4,128,256]{2,1,0:T(8,128)S(1)} fusion(f32[4,128,256]{2,1,0:T(8,128)S(1)} %fusion.30, f32[4,128,256]{1,2,0:T(8,128)S(1)} %convolution_bitcast_fusion, f32[4,128,256]{1,2,0:T(8,128)S(1)} %fusion.1, f32[128,256]{0,1:T(8,128)S(1)} %get-tuple-element.8, f32[128,256]{0,1:T(8,128)S(1)} %get-tuple-element.9), kind=kOutput, calls=%fused_computation.8 | convolution fusion | flops 404094976 | bytes 2359296 | tf_op jit(solution)/shard_map/bks,st->bkt/dot_general | solution.py:22
  67.0 1.9 %fusion.24 = f32[4,128,256]{1,2,0:T(8,128)S(1)} fusion(f32[4,128,256]{2,1,0:T(8,128)S(1)} %convolution_subtract_fusion.1, f32[4,128,256]{2,1,0:T(8,128)S(1)} %convolution_add_fusion.1, f32[128,256]{1,0:T(8,128)S(1)} %convolution_subtract_fusion.3, f32[128,256]{1,0:T(8,128)S(1)} %convolution_add_fusion.2), kind=kOutput, calls=%fused_computation.49 | convolution fusion | flops 403963904 | bytes 1835008 | tf_op jit(solution)/shard_map/bks,st->bkt/dot_general | solution.py:22
  69.0 1.7 %fusion.26 = f32[4,128,256]{1,2,0:T(8,128)S(1)} fusion(f32[4,128,256]{2,1,0:T(8,128)S(1)} %convolution_subtract_fusion.1, f32[4,128,256]{2,1,0:T(8,128)S(1)} %convolution_add_fusion.1, f32[128,256]{1,0:T(8,128)S(1)} %convolution_subtract_fusion.3, f32[128,256]{1,0:T(8,128)S(1)} %convolution_add_fusion.2), kind=kOutput, calls=%fused_computation.51 | convolution fusion | flops 403963904 | bytes 1835008 | tf_op jit(solution)/shard_map/bks,st->bkt/dot_general | solution.py:22
  70.7 1.7 %convolution_add_fusion = f32[4,128,256]{1,2,0:T(8,128)S(1)} fusion(f32[4,128,256]{1,2,0:T(8,128)S(1)} %fusion.24, f32[4,128,256]{2,1,0:T(8,128)S(1)} %convolution_subtract_fusion.1, f32[4,128,256]{2,1,0:T(8,128)S(1)} %convolution_add_fusion.1, f32[128,256]{1,0:T(8,128)S(1)} %convolution_subtract_fusion.3, f32[128,256]{1,0:T(8,128)S(1)} %convolution_add_fusion.2), kind=kOutput, calls=%fused_computation.5 | convolution fusion | flops 404094976 | bytes 2359296 | tf_op jit(solution)/shard_map/bks,st->bkt/dot_general | solution.py:22
  72.4 1.7 %convolution_subtract_fusion = f32[4,128,256]{1,2,0:T(8,128)S(1)} fusion(f32[4,128,256]{1,2,0:T(8,128)S(1)} %fusion.26, f32[4,128,256]{2,1,0:T(8,128)S(1)} %convolution_subtract_fusion.1, f32[4,128,256]{2,1,0:T(8,128)S(1)} %convolution_add_fusion.1, f32[128,256]{1,0:T(8,128)S(1)} %convolution_subtract_fusion.3, f32[128,256]{1,0:T(8,128)S(1)} %convolution_add_fusion.2), kind=kOutput, calls=%fused_computation.6 | convolution fusion | flops 404094976 | bytes 2359296 | tf_op jit(solution)/shard_map/bks,st->bkt/dot_general | solution.py:22
  74.1 0.0 copy-done.3
  74.2 0.8 fusion.10
  74.9 1.5 %fusion.3 = f32[4,64,256]{2,1,0:T(8,128)} fusion(f32[4,256,64]{1,2,0:T(8,128)S(1)} %fusion.10, f32[4,128,256]{1,2,0:T(8,128)S(1)} %convolution_subtract_fusion, f32[4,128,256]{1,2,0:T(8,128)S(1)} %convolution_add_fusion, f32[128,256]{0,1:T(8,128)S(1)} %get-tuple-element.8, f32[128,256]{0,1:T(8,128)S(1)} %get-tuple-element.9, f32[128,128]{0,1:T(8,128)S(1)} %copy-done.5), kind=kOutput, calls=%fused_computation.11 | convolution fusion | flops 101187584 | bytes 1900544 | tf_op jit(solution)/shard_map/kn,bns->bks/dot_general | solution.py:18
  76.4 1.0 reshape.149
  77.4 0.1 add_convert_fusion
  77.5 0.1 copy.49
  77.6 18.3 %all_to_all.23 = bf16[4,128,128]{2,0,1:T(4,128)(2,1)S(1)} all-to-all(bf16[4,128,128]{2,0,1:T(4,128)(2,1)S(1)} %copy.49), channel_id=1, replica_groups=mesh['ctx'=128,'tp'=4] {'ctx'}, dimensions={1} | all-to-all | bytes 262144 | tf_op jit(solution)/shard_map/all_to_all | solution.py:126
  95.9 1.3 fusion
  97.2 0.0 reduce-scatter.2.cloned.1.call-update
  97.2 34.2 %reduce-scatter.2.cloned.1.call-done = bf16[512,128]{0,1:T(8,128)(2,1)} async-done(((bf16[2048,128]{0,1:T(8,128)(2,1)}), bf16[512,128]{0,1:T(8,128)(2,1)}) %reduce-scatter.2.cloned.1.call-update) | async-done | bytes 131088 | tf_op jit(solution)/shard_map/reduce_scatter | solution.py:128
  131.4 1.7 %copy.50 = bf16[512,128]{1,0:T(8,128)(2,1)} copy(bf16[512,128]{0,1:T(8,128)(2,1)} %reduce-scatter.2.cloned.1.call-done) | data formatting | bytes 262144 | tf_op jit(solution)/shard_map/reduce_scatter | solution.py:128
  (15 shorter events, 0.1 us)
Async XLA Ops:
  6.5 89.4 %copy-start = (bf16[512,2048]{1,0:T(8,128)(2,1)S(1)}, bf16[512,2048]{1,0:T(8,128)(2,1)}, u32[]{:S(2)}) copy-start(bf16[512,2048]{1,0:T(8,128)(2,1)} %param.9) | copy-start | bytes 6291460
  8.6 12.4 %collective-permute-start = (bf16[3,512,2]{2,1,0:T(8,128)(2,1)}, bf16[3,512,2]{2,1,0:T(8,128)(2,1)S(1)}, u32[]{:S(2)}, u32[]{:S(2)}) collective-permute-start(bf16[3,512,2]{2,1,0:T(8,128)(2,1)} %slice.49), channel_id=1, source_target_pairs={{0,4},{4,8},{8,12},{12,16},{16,20},{20,24},{24,28},{28,32},{32,36}... | collective-permute-start | bytes 18440 | tf_op jit(solution)/shard_map/ppermute | solution.py:14
  12.8 6.4 %copy-start.2 = (f32[128,128]{0,1:T(8,128)}, f32[128,128]{0,1:T(8,128)S(1)}, u32[]{:S(2)}) copy-start(f32[128,128]{0,1:T(8,128)S(1)} %fusion.85) | copy-start | bytes 196612
  13.1 1.8 %copy-start.4 = (f32[128,128]{0,1:T(8,128)}, f32[128,128]{0,1:T(8,128)S(1)}, u32[]{:S(2)}) copy-start(f32[128,128]{0,1:T(8,128)S(1)} %fusion.84) | copy-start | bytes 196612
  14.6 4.6 %copy-start.6 = (f32[1,128,256]{1,2,0:T(8,128)}, f32[1,128,256]{1,2,0:T(8,128)S(1)}, u32[]{:S(2)}) copy-start(f32[1,128,256]{1,2,0:T(8,128)S(1)} %fusion.4) | copy-start | bytes 393220
  14.9 4.3 %copy-start.7 = (f32[1,128,256]{1,2,0:T(8,128)}, f32[1,128,256]{1,2,0:T(8,128)S(1)}, u32[]{:S(2)}) copy-start(f32[1,128,256]{1,2,0:T(8,128)S(1)} %convolution_bitcast_fusion.1) | copy-start | bytes 393220
  16.7 4.3 %copy-start.8 = (f32[3,3,512]{2,1,0:T(4,128)S(1)}, f32[3,3,512]{2,1,0:T(4,128)}, u32[]{:S(2)}) copy-start(f32[3,3,512]{2,1,0:T(4,128)} %param.6) | copy-start | bytes 55300
  16.7 4.3 %copy-start.1 = (bf16[3,512,128]{2,1,0:T(8,128)(2,1)S(1)}, bf16[3,512,128]{2,1,0:T(8,128)(2,1)}, u32[]{:S(2)}) copy-start(bf16[3,512,128]{2,1,0:T(8,128)(2,1)} %param.5) | copy-start | bytes 1179652
  23.3 31.3 %all-to-all-start = ((bf16[128,4,128]{2,1,0:T(4,128)(2,1)}), bf16[128,4,128]{2,1,0:T(4,128)(2,1)S(1)}, u32[]{:S(2)}, u32[]{:S(2)}) async-start(bf16[128,4,128]{2,1,0:T(4,128)(2,1)} %bitcast.4), calls=%async_computation | async-start | bytes 262144 | tf_op jit(solution)/shard_map/all_to_all | solution.py:109
  43.3 88.0 %reduce-scatter.2.cloned.1.call-start = ((), (), s32[]{:S(2)}) async-start(), calls=%async_computation.3 | async-start | bytes 655360 | tf_op jit(solution)/shard_map/reduce_scatter | solution.py:128
  72.4 1.8 %copy-start.3 = (f32[128,128]{0,1:T(8,128)S(1)}, f32[128,128]{0,1:T(8,128)}, u32[]{:S(2)}) copy-start(f32[128,128]{0,1:T(8,128)} %copy-done.2) | copy-start | bytes 196612
  72.4 2.5 %copy-start.5 = (f32[128,128]{0,1:T(8,128)S(1)}, f32[128,128]{0,1:T(8,128)}, u32[]{:S(2)}) copy-start(f32[128,128]{0,1:T(8,128)} %copy-done.4) | copy-start | bytes 196612
Sparse Core Ops, SparseCore 0:
  97.3 34.0 reduce-scatter.1
where the time goes:
time: 140 us
  waiting for transfers between devices  41 us (29%)
  matrix products  30.2 us (22%)
  starting transfers between devices  24.2 us (17%)
  blocking collectives  18.3 us (13%)
  between operations  13.7 us (10%)
  local copies, waits for them, and re-layouts  9.05 us (6%)
  other arithmetic  3.38 us (2%)
    reduce_scatter x1, waiting for transfers between devices, local(): lax.psum_scatter(lax.dot_general(out_weight, gated, (((0,), (0,)), ((), (...  34.2 us
    dot_general x12, matrix products, right_product(): return jnp.einsum('bks,st->bkt', stacked, matrix, precision=highest)  23.5 us
    all_to_all x1, starting transfers between devices, local(): lax.all_to_all(product, 'ctx', split_axis=0, concat_axis=1, tiled=True)  20.1 us
    all_to_all x1, blocking collectives, local(): lax.all_to_all(long_mix, 'ctx', split_axis=1, concat_axis=0, tiled=True)  18.3 us
    all_to_all x1, waiting for transfers between devices, local(): lax.all_to_all(product, 'ctx', split_axis=0, concat_axis=1, tiled=True)  6.82 us
    dot_general x6, matrix products, left_product(): return jnp.einsum('kn,bns->bks', matrix, stacked, precision=highest)  5.45 us
    ppermute x1, starting transfers between devices, from_behind(): lax.ppermute(value, axis, [(source, source + steps) for source in range(i...  3.94 us
  transfers between devices with their start and end apart: 3, of which 2 were waited for; matrix products, arithmetic and copies ran while one was open for 9% of the time, Pallas kernels for 0%

commit v1 on v0

--- a/solution.py
+++ b/solution.py
@@ -106,7 +106,10 @@
         )
     query_conv = conv_all[0]
     product = (conv_all[1] * conv_all[2]).astype(jnp.bfloat16)
-    gathered = lax.all_to_all(product, "ctx", split_axis=0, concat_axis=1, tiled=True)
+    gathered = jnp.concatenate(
+        lax.all_to_all(jnp.stack(jnp.split(product, lax.axis_size("ctx"), axis=0)), "ctx", 0, 0),
+        axis=1,
+    )
     signal = gathered.astype(jnp.float32)
     sig_real, sig_imag = forward_dft(signal.reshape(chan_dev, half_rows, col_count), tables)
     four_shape = (group_dev, per_group, row_count, col_count)

time: 140 us -> 211 us (1.51)
  local copies, waits for them, and re-layouts: 9.05 us -> 80.6 us
    unnamed x18 -> x145, local copies, waits for them, and re-layouts: 0.04 us -> 71.7 us
  transfers between devices with their start and end apart: 3 -> 3, of which waited for: 2 -> 2; matrix products, arithmetic and copies ran while one was open for 9% -> 6% of each run, Pallas kernels for 0% -> 0%
where the time goes in v1:
time: 211 us
  local copies, waits for them, and re-layouts  80.6 us (38%)
  waiting for transfers between devices  41 us (19%)
  matrix products  30.2 us (14%)
  starting transfers between devices  24 us (11%)
  blocking collectives  18.3 us (9%)
  between operations  13.8 us (7%)
  other arithmetic  2.72 us (1%)
    unnamed x145, local copies, waits for them, and re-layouts  71.7 us
    reduce_scatter x1, waiting for transfers between devices, local(): lax.psum_scatter(lax.dot_general(out_weight, gated, (((0,), (0,)), ((), (...  34.2 us
    dot_general x12, matrix products, right_product(): return jnp.einsum('bks,st->bkt', stacked, matrix, precision=highest)  23.5 us
    all_to_all x1, starting transfers between devices, local(): lax.all_to_all(jnp.stack(jnp.split(product, lax.axis_size('ctx'), axis=0)...  19.8 us
    all_to_all x1, blocking collectives, local(): lax.all_to_all(long_mix, 'ctx', split_axis=1, concat_axis=0, tiled=True)  18.3 us
    all_to_all x1, waiting for transfers between devices, local(): lax.all_to_all(jnp.stack(jnp.split(product, lax.axis_size('ctx'), axis=0)...  6.83 us
    dot_general x6, matrix products, left_product(): return jnp.einsum('kn,bns->bks', matrix, stacked, precision=highest)  5.45 us
  transfers between devices with their start and end apart: 3, of which 2 were waited for; matrix products, arithmetic and copies ran while one was open for 6% of the time, Pallas kernels for 0%

profile of v1, /device:TPU:1, one launch (start us, length us, event | category | flops | bytes accessed | tf_op | source)
XLA Modules:
  0.0 210.6 jit_solution(17544458526883891699)
XLA Ops:
  6.5 1.3 slice.177
  7.9 4.0 %collective-permute-start = (bf16[3,512,2]{2,1,0:T(8,128)(2,1)S(1)}, bf16[3,512,2]{2,1,0:T(8,128)(2,1)S(1)}, u32[]{:S(2)}, u32[]{:S(2)}) collective-permute-start(bf16[3,512,2]{2,1,0:T(8,128)(2,1)S(1)} %slice.177), channel_id=1, source_target_pairs={{0,4},{4,8},{8,12},{12,16},{16,20},{20,24},{24,28},{28,32},{32,36}... | collective-permute-start | bytes 18440 | tf_op jit(solution)/shard_map/ppermute | solution.py:14
  12.4 1.2 dynamic-slice_reduce_fusion
  14.2 1.8 fusion.46
  16.0 2.5 %fusion.50 = f32[128,256]{1,0:T(8,128)} fusion(f32[1,128,256]{1,2,0:T(8,128)S(1)} %fusion.4, f32[1,128,256]{1,2,0:T(8,128)S(1)} %convolution_bitcast_fusion.1), kind=kOutput, calls=%fused_computation.209 | convolution fusion | flops 102137856 | bytes 393216 | tf_op jit(solution)/shard_map/bks,st->bkt/dot_general | solution.py:22
  18.5 1.8 convolution_subtract_fusion.3
  20.7 1.2 fusion.5
  22.5 0.6 constant_dynamic-update-slice_fusion.126
  23.6 0.6 constant_dynamic-update-slice_fusion.124
  24.7 0.6 constant_dynamic-update-slice_fusion.122
  25.9 0.6 constant_dynamic-update-slice_fusion.120
  27.0 0.6 constant_dynamic-update-slice_fusion.118
  28.1 0.6 constant_dynamic-update-slice_fusion.116
  29.2 0.6 constant_dynamic-update-slice_fusion.114
  30.4 0.6 constant_dynamic-update-slice_fusion.112
  31.5 0.6 constant_dynamic-update-slice_fusion.110
  32.6 0.6 constant_dynamic-update-slice_fusion.108
  33.8 0.6 constant_dynamic-update-slice_fusion.106
  34.9 0.6 constant_dynamic-update-slice_fusion.104
  36.0 0.6 constant_dynamic-update-slice_fusion.102
  37.2 0.6 constant_dynamic-update-slice_fusion.100
  38.3 0.6 constant_dynamic-update-slice_fusion.98
  39.4 0.6 constant_dynamic-update-slice_fusion.96
  40.5 0.6 constant_dynamic-update-slice_fusion.94
  41.7 0.6 constant_dynamic-update-slice_fusion.92
  94.2 19.8 %all-to-all-start = ((bf16[128,4,128]{2,1,0:T(4,128)(2,1)}), bf16[128,4,128]{2,1,0:T(4,128)(2,1)S(1)}, u32[]{:S(2)}, u32[]{:S(2)}) async-start(bf16[128,4,128]{2,1,0:T(4,128)(2,1)} %constant_dynamic-update-slice_fusion), calls=%async_computation | async-start | bytes 262144 | tf_op jit(solution)/shard_map/all_to_all | solution.py:110
  114.8 0.8 dynamic_slice.7
  115.6 2.8 %convolution_add_fusion.2 = f32[128,256]{1,0:T(8,128)S(1)} fusion(f32[128,256]{1,0:T(8,128)} %fusion.50, f32[1,128,256]{1,2,0:T(8,128)} %copy-done.7, f32[1,128,256]{1,2,0:T(8,128)} %copy-done.6), kind=kOutput, calls=%fused_computation.13 | convolution fusion | flops 102170624 | bytes 524288 | tf_op jit(solution)/shard_map/bks,st->bkt/dot_general | solution.py:22
  118.5 6.8 %all-to-all-done = bf16[128,4,128]{2,1,0:T(4,128)(2,1)S(1)} async-done(((bf16[128,4,128]{2,1,0:T(4,128)(2,1)}), bf16[128,4,128]{2,1,0:T(4,128)(2,1)S(1)}, u32[]{:S(2)}, u32[]{:S(2)}) %all-to-all-start) | async-done | bytes 131104 | tf_op jit(solution)/shard_map/all_to_all | solution.py:110
  125.3 0.7 copy.108
  126.0 1.6 reshape.401
  127.5 1.3 fusion.1
  128.9 1.3 convolution_bitcast_fusion
  130.2 1.9 fusion.28
  132.1 1.9 fusion.30
  134.0 1.9 convolution_subtract_fusion.1
  135.9 1.9 convolution_add_fusion.1
  137.8 1.9 fusion.24
  139.7 1.7 fusion.26
  141.4 1.7 convolution_add_fusion
  143.2 1.7 convolution_subtract_fusion
  144.9 0.8 fusion.10
  145.7 1.5 fusion.3
  147.1 1.0 reshape.405
  148.3 18.3 %all_to_all.15 = bf16[4,128,128]{2,0,1:T(4,128)(2,1)S(1)} all-to-all(bf16[4,128,128]{2,0,1:T(4,128)(2,1)S(1)} %copy.89), channel_id=1, replica_groups=mesh['ctx'=128,'tp'=4] {'ctx'}, dimensions={1} | all-to-all | bytes 262144 | tf_op jit(solution)/shard_map/all_to_all | solution.py:129
  166.6 1.3 fusion
  167.9 34.2 %reduce-scatter.2.cloned.1.call-done = bf16[512,128]{0,1:T(8,128)(2,1)} async-done(((bf16[2048,128]{0,1:T(8,128)(2,1)}), bf16[512,128]{0,1:T(8,128)(2,1)}) %reduce-scatter.2.cloned.1.call-update) | async-done | bytes 131088 | tf_op jit(solution)/shard_map/reduce_scatter | solution.py:131
  202.1 1.7 copy.90
  (143 shorter events, 64.5 us)
Async XLA Ops:
  6.5 160.1 %copy-start = (bf16[512,2048]{1,0:T(8,128)(2,1)S(1)}, bf16[512,2048]{1,0:T(8,128)(2,1)}, u32[]{:S(2)}) copy-start(bf16[512,2048]{1,0:T(8,128)(2,1)} %param.9) | copy-start | bytes 6291460
  7.9 12.5 %collective-permute-start = (bf16[3,512,2]{2,1,0:T(8,128)(2,1)S(1)}, bf16[3,512,2]{2,1,0:T(8,128)(2,1)S(1)}, u32[]{:S(2)}, u32[]{:S(2)}) collective-permute-start(bf16[3,512,2]{2,1,0:T(8,128)(2,1)S(1)} %slice.177), channel_id=1, source_target_pairs={{0,4},{4,8},{8,12},{12,16},{16,20},{20,24},{24,28},{28,32},{32,36}... | collective-permute-start | bytes 18440 | tf_op jit(solution)/shard_map/ppermute | solution.py:14
  12.1 2.0 copy-start.2
  12.4 1.8 copy-start.4
  13.9 4.6 %copy-start.6 = (f32[1,128,256]{1,2,0:T(8,128)}, f32[1,128,256]{1,2,0:T(8,128)S(1)}, u32[]{:S(2)}) copy-start(f32[1,128,256]{1,2,0:T(8,128)S(1)} %fusion.4) | copy-start | bytes 393220
  14.2 4.3 %copy-start.7 = (f32[1,128,256]{1,2,0:T(8,128)}, f32[1,128,256]{1,2,0:T(8,128)S(1)}, u32[]{:S(2)}) copy-start(f32[1,128,256]{1,2,0:T(8,128)S(1)} %convolution_bitcast_fusion.1) | copy-start | bytes 393220
  16.0 4.3 %copy-start.8 = (f32[3,3,512]{2,1,0:T(4,128)S(1)}, f32[3,3,512]{2,1,0:T(4,128)}, u32[]{:S(2)}) copy-start(f32[3,3,512]{2,1,0:T(4,128)} %param.6) | copy-start | bytes 55300
  16.0 4.3 %copy-start.1 = (bf16[3,512,128]{2,1,0:T(8,128)(2,1)S(1)}, bf16[3,512,128]{2,1,0:T(8,128)(2,1)}, u32[]{:S(2)}) copy-start(bf16[3,512,128]{2,1,0:T(8,128)(2,1)} %param.5) | copy-start | bytes 1179652
  94.2 31.1 %all-to-all-start = ((bf16[128,4,128]{2,1,0:T(4,128)(2,1)}), bf16[128,4,128]{2,1,0:T(4,128)(2,1)S(1)}, u32[]{:S(2)}, u32[]{:S(2)}) async-start(bf16[128,4,128]{2,1,0:T(4,128)(2,1)} %constant_dynamic-update-slice_fusion), calls=%async_computation | async-start | bytes 262144 | tf_op jit(solution)/shard_map/all_to_all | solution.py:110
  114.1 88.0 %reduce-scatter.2.cloned.1.call-start = ((), (), s32[]{:S(2)}) async-start(), calls=%async_computation.3 | async-start | bytes 655360 | tf_op jit(solution)/shard_map/reduce_scatter | solution.py:131
  143.1 1.8 copy-start.3
  143.1 2.5 %copy-start.5 = (f32[128,128]{0,1:T(8,128)S(1)}, f32[128,128]{0,1:T(8,128)}, u32[]{:S(2)}) copy-start(f32[128,128]{0,1:T(8,128)} %copy-done.4) | copy-start | bytes 196612
Sparse Core Ops, SparseCore 0:
  168.0 34.0 reduce-scatter.1
